TPU v7x, 32 devices: a whole 2x2x4 slice. The times are simulated.
32 devices in a mesh: groups: 2 (over y), wide: 4 (over z), narrow: 4 (over x, core).
Axes of the slice: x: 2, y: 2, z: 4, core: 2. Of those that a mesh axis runs over, the one named last changes fastest.
Arguments:
- target_states: bfloat16 [256, 8192], P(('groups', 'wide'), 'narrow'), parts along dimension 0, may hold values from -6 to 6
- source_states: bfloat16 [256, 8192], P(('groups', 'wide'), 'narrow'), parts along dimension 0, may hold values from -6 to 6
- target_gate: bfloat16 [8192, 14336], P('narrow', 'wide'), may hold values from -0.0625 to 0.0625
- target_up: bfloat16 [8192, 14336], P('narrow', 'wide'), may hold values from -0.0625 to 0.0625
- source_gate: bfloat16 [8192, 14336], P('narrow', 'wide'), may hold values from -0.0625 to 0.0625
- source_up: bfloat16 [8192, 14336], P('narrow', 'wide'), may hold values from -0.0625 to 0.0625
- token_ids: int32 [256], P(('groups', 'narrow')), parts along dimension 0, may hold values from 0 to 128255
- lengths: int32 [16], P(('groups', 'narrow')), parts along dimension 0, may hold values from 1 to 16
- ratio_weight: float32 [128256], replicated, may hold values from 0.25 to 1
Outputs:
- target_hidden: bfloat16 [256, 14336], P(('groups', 'narrow'), 'wide'), parts along dimension 0
- ratio_hidden: bfloat16 [256, 14336], P(('groups', 'narrow'), 'wide'), parts along dimension 0
There are 2 independent parts, one for each index of `groups`. A program takes and returns all parts, laid end to end along the dimension named above; an argument that names none is the same for every part. Nothing has to cross between parts.
All inputs are finite; a program needn't handle non-finite values.
Results may differ from a plain program's by a relative error of at most 0.02.
Values may be sent and summed in bfloat16 or wider, within the bound.
A program may use at most 128 MiB of HBM per device.

v0:
```python
import functools

import jax
import jax.numpy as jnp
from jax import lax
from jax.experimental import pallas as pl
from jax.experimental.pallas import tpu as pltpu
from jax.sharding import PartitionSpec as P

MESH = pl.DeviceIdType.MESH
VMEM_BYTES = 67_000_000


def matmul(left, right):
    return jnp.dot(left, right, preferred_element_type=jnp.float32)


def pair_project(w_gate, w_upper, piece):
    return jnp.concatenate([matmul(piece, w_gate), matmul(piece, w_upper)], axis=1)


def gated(summed, hidden_cols):
    return jax.nn.silu(summed[:, :hidden_cols]) * summed[:, hidden_cols:]


def kernel(
    wide, tn, slots,
    ids_ref, len_ref, table_ref, ts_ref, ss_ref, tg_ref, tu_ref, sg_ref, su_ref,
    t_out, r_out,
    gath, wbuf, part, a_send, a_recv, b_send, b_recv, kept,
    live_ref, weight_ref, table, table_sem, own_sem, g_send, g_recv, w_sem, as_sem, ar_sem, bs_sem, br_sem,
):
    w = lax.axis_index("wide")
    n = lax.axis_index("narrow")
    x = n // 2
    c = n % 2
    mate = 2 * x + (1 - c)
    across = 2 * (1 - x) + c
    cols = tg_ref.shape[1]
    per = cols // tn
    units = 2 * per
    rows = part.shape[3]

    def weight_copies(slot, model, j):
        pair = (tg_ref, tu_ref) if model == 0 else (sg_ref, su_ref)
        span = pl.ds(pl.multiple_of(j * tn, tn), tn)
        return [
            pltpu.make_async_copy(pair[k].at[:, span], wbuf.at[slot, k], w_sem.at[slot, k])
            for k in range(2)
        ]

    def load(u):
        slot = u % slots

        @pl.when(u < per)
        def _():
            for copy in weight_copies(slot, 0, u):
                copy.start()

        @pl.when(jnp.logical_and(u >= per, u < units))
        def _():
            for copy in weight_copies(slot, 1, u - per):
                copy.start()

    own = [
        pltpu.make_async_copy(ref, gath.at[m, w], own_sem.at[m])
        for m, ref in enumerate((ts_ref, ss_ref))
    ]
    for copy in own:
        copy.start()

    def load_ahead(first, last):
        for u in range(first, min(last, slots, units)):
            for copy in weight_copies(u, u // per, u % per):
                copy.start()

    load_ahead(0, 1)
    fetch = pltpu.make_async_copy(table_ref, table, table_sem)
    barrier = pltpu.get_barrier_semaphore()

    def greet(axis, index):
        pl.semaphore_signal(barrier, inc=1, device_id={axis: index}, device_id_type=MESH)

    greet("narrow", mate)
    greet("narrow", across)

    @pl.when(w > 0)
    def _():
        greet("wide", w - 1)

    @pl.when(w < wide - 1)
    def _():
        greet("wide", w + 1)

    inner = jnp.logical_and(w > 0, w < wide - 1)
    pl.semaphore_wait(barrier, jnp.where(inner, 4, 3))

    def hop(m, block, up):
        return pltpu.make_async_remote_copy(
            src_ref=gath.at[m, block],
            dst_ref=gath.at[m, block],
            send_sem=g_send.at[m, 0 if up else 1, block],
            recv_sem=g_recv.at[m, block],
            device_id={"wide": w + 1 if up else w - 1},
            device_id_type=MESH,
        )

    def gather_step(m, s):
        @pl.when(w - s >= 0)
        def _():
            if s > 0:
                hop(m, w - s, True).wait_recv()

            @pl.when(w < wide - 1)
            def _():
                hop(m, w - s, True).start()

        @pl.when(w + s <= wide - 1)
        def _():
            if s > 0:
                hop(m, w + s, False).wait_recv()

            @pl.when(w > 0)
            def _():
                hop(m, w + s, False).start()

        if m == 0:
            @pl.when(jnp.logical_and(w == s, w < wide - 1))
            def _():
                hop(1, w, True).start()

            @pl.when(jnp.logical_and(wide - 1 - w == s, w > 0))
            def _():
                hop(1, w, False).start()

    for copy in own:
        copy.wait()
    batch = pl.cdiv(slots - 1, wide)
    for s in range(wide):
        gather_step(0, s)
        load_ahead(1 + s * batch, 1 + (s + 1) * batch)
    fetch.start()

    def a_copy(u):
        return pltpu.make_async_remote_copy(
            src_ref=a_send.at[u], dst_ref=a_recv.at[u],
            send_sem=as_sem.at[u], recv_sem=ar_sem.at[u],
            device_id={"narrow": mate}, device_id_type=MESH,
        )

    def b_copy(u):
        return pltpu.make_async_remote_copy(
            src_ref=b_send.at[u], dst_ref=b_recv.at[u],
            send_sem=bs_sem.at[u], recv_sem=br_sem.at[u],
            device_id={"narrow": across}, device_id_type=MESH,
        )

    def cross(u):
        a_copy(u).wait_recv()
        for k in range(2):
            total = part[u, k, across] + a_recv[u, 1 - x, k].astype(jnp.float32)
            b_send[u, k] = total.astype(jnp.bfloat16)
        b_copy(u).start()

    def unit(u, carry):
        for s in range(1, wide):
            @pl.when(u == min(1 + 2 * s, per))
            def _():
                gather_step(1, s)

        slot = u % slots
        model = u // per
        left = gath[model].reshape(4 * rows, gath.shape[3])
        for k in range(2):
            weight_copies(slot, 0, 0)[k].wait()
            part[u, k] = matmul(left, wbuf[slot, k]).reshape(4, rows, tn)
        for i in range(2):
            for k in range(2):
                a_send[u, i, k] = part[u, k, 2 * i + 1 - c].astype(jnp.bfloat16)
        a_copy(u).start()

        @pl.when(u > 0)
        def _():
            cross(u - 1)

        load(u + slots)
        return carry

    lax.fori_loop(0, units, unit, 0)
    cross(units - 1)

    fetch.wait()
    row = lax.broadcasted_iota(jnp.int32, (rows, 1), 0)
    hlen = rows // len_ref.shape[0]
    lived = jnp.zeros((rows, 1), jnp.float32)
    for h in range(len_ref.shape[0]):
        inside = jnp.logical_and(row >= h * hlen, row < h * hlen + len_ref[h])
        lived = jnp.where(inside, 1.0, lived)
    weights = jnp.zeros((rows, 1), jnp.float32)
    for i in range(rows):
        weights = jnp.where(row == i, table[ids_ref[i]], weights)
    live_ref[...] = lived
    weight_ref[...] = weights

    def summed(u, k):
        near = part[u, k, n] + a_recv[u, x, k].astype(jnp.float32)
        return near + b_recv[u, k].astype(jnp.float32)

    def activation(u):
        b_copy(u).wait_recv()
        gate = summed(u, 0)
        return gate / (1.0 + jnp.exp(-gate)) * summed(u, 1)

    def finish_target(j, carry):
        act = activation(j)
        kept[j] = act
        t_out[:, pl.ds(pl.multiple_of(j * tn, tn), tn)] = (live_ref[...] * act).astype(t_out.dtype)
        return carry

    def finish_ratio(j, carry):
        act = activation(per + j)
        ratio = live_ref[...] * (kept[j] - weight_ref[...] * act)
        r_out[:, pl.ds(pl.multiple_of(j * tn, tn), tn)] = ratio.astype(r_out.dtype)
        return carry

    lax.fori_loop(0, per, finish_target, 0)
    lax.fori_loop(0, per, finish_ratio, 0)

    def drain(u, carry):
        a_copy(u).wait_send()
        b_copy(u).wait_send()
        return carry

    lax.fori_loop(0, units, drain, 0)
    for m in range(2):
        for block in range(wide):
            @pl.when(jnp.logical_and(block <= w, w < wide - 1))
            def _():
                hop(m, block, True).wait_send()

            @pl.when(jnp.logical_and(block >= w, w > 0))
            def _():
                hop(m, block, False).wait_send()


def hand_over(*refs):
    taken, given, held, in_sem, out_sem = refs[:2], refs[2:4], refs[4], refs[5], refs[6]
    arrive = [pltpu.make_async_copy(taken[i], held.at[i], in_sem.at[i]) for i in range(2)]
    leave = [pltpu.make_async_copy(held.at[i], given[i], out_sem.at[i]) for i in range(2)]
    for copy in arrive:
        copy.start()
    for i in range(2):
        arrive[i].wait()
        leave[i].start()
    for copy in leave:
        copy.wait()


def plan(states, weights, wide, narrow):
    cols = weights.shape[1]
    tokens = states.shape[0] * wide
    if narrow != 4 or wide < 2 or tokens % 64 or states.shape[0] % 16:
        return None
    for tn in (512, 256):
        if cols % tn:
            continue
        units = 2 * cols // tn
        unit_bytes = tn * tokens * 2 * (4 + 1 + 1 + 1)
        fixed = 2 * tokens * states.shape[1] * 2 + cols * tokens * 4 + units * unit_bytes
        slots = (VMEM_BYTES - 8_000_000 - fixed) // (4 * tn * states.shape[1])
        slots = min(slots, units, 1 + 2 * wide)
        if slots >= 2:
            return tn, slots
    return None


def fused(states, weights, token_ids, lengths, ratio_weight, wide, tn, slots):
    rows = states[0].shape[0] * wide // 4
    depth = states[0].shape[1]
    cols = weights[0].shape[1]
    units = 2 * cols // tn
    smem = pl.BlockSpec(memory_space=pltpu.SMEM)
    vmem = pl.BlockSpec(memory_space=pltpu.VMEM)
    hbm = pl.BlockSpec(memory_space=pl.ANY)
    out = jax.ShapeDtypeStruct((rows, cols), jnp.bfloat16)
    dma = pltpu.SemaphoreType.DMA
    pair = pl.pallas_call(
        functools.partial(kernel, wide, tn, slots),
        out_shape=(out, out),
        in_specs=[smem, smem] + [hbm] * 7,
        out_specs=(vmem, vmem),
        scratch_shapes=[
            pltpu.VMEM((2, wide, states[0].shape[0], depth), jnp.bfloat16),
            pltpu.VMEM((slots, 2, depth, tn), jnp.bfloat16),
            pltpu.VMEM((units, 2, 4, rows, tn), jnp.float32),
            pltpu.VMEM((units, 2, 2, rows, tn), jnp.bfloat16),
            pltpu.VMEM((units, 2, 2, rows, tn), jnp.bfloat16),
            pltpu.VMEM((units, 2, rows, tn), jnp.bfloat16),
            pltpu.VMEM((units, 2, rows, tn), jnp.bfloat16),
            pltpu.VMEM((units // 2, rows, tn), jnp.float32),
            pltpu.VMEM((rows, 1), jnp.float32),
            pltpu.VMEM((rows, 1), jnp.float32),
            pltpu.SMEM(ratio_weight.shape, jnp.float32),
            dma,
            dma((2,)),
            dma((2, 2, wide)),
            dma((2, wide)),
            dma((slots, 2)),
            dma((units,)),
            dma((units,)),
            dma((units,)),
            dma((units,)),
        ],
        compiler_params=pltpu.CompilerParams(
            collective_id=0, has_side_effects=True, vmem_limit_bytes=VMEM_BYTES
        ),
        name="rescore",
    )(token_ids, lengths, ratio_weight, *states, *weights)
    return pl.pallas_call(
        hand_over,
        out_shape=(out, out),
        in_specs=[hbm, hbm],
        out_specs=(hbm, hbm),
        scratch_shapes=[pltpu.VMEM((2, rows, cols), jnp.bfloat16), dma((2,)), dma((2,))],
        name="hand_over",
    )(*pair)


def local(
    wide,
    narrow,
    target_states,
    source_states,
    target_gate,
    target_up,
    source_gate,
    source_up,
    token_ids,
    lengths,
    ratio_weight,
):
    hidden_cols = target_gate.shape[1]
    own_rows = token_ids.shape[0]
    chosen = plan(target_states, target_gate, wide, narrow)
    if chosen is not None:
        return fused(
            (target_states, source_states),
            (target_gate, target_up, source_gate, source_up),
            token_ids,
            lengths,
            ratio_weight,
            wide,
            *chosen,
        )
    slot_count = own_rows // lengths.shape[0]
    slots = jnp.arange(slot_count, dtype=jnp.int32)
    live = (slots[None, :] < lengths[:, None]).reshape(-1).astype(jnp.float32)
    weight = ratio_weight[token_ids]
    target_terms = pair_project(
        target_gate, target_up, lax.all_gather(target_states, "wide", axis=0, tiled=True)
    )
    source_terms = pair_project(
        source_gate, source_up, lax.all_gather(source_states, "wide", axis=0, tiled=True)
    )
    target_sum, source_sum = (
        lax.psum_scatter(
            target_terms.astype(jnp.bfloat16), "narrow", scatter_dimension=0, tiled=True
        ).astype(jnp.float32),
        lax.psum_scatter(
            source_terms.astype(jnp.bfloat16), "narrow", scatter_dimension=0, tiled=True
        ).astype(jnp.float32),
    )
    target_act = gated(target_sum, hidden_cols)
    source_act = gated(source_sum, hidden_cols)
    target_out = (live[:, None] * target_act).astype(jnp.bfloat16)
    ratio_out = (live[:, None] * (target_act - weight[:, None] * source_act)).astype(jnp.bfloat16)
    return (target_out, ratio_out)


def solution(mesh):
    placed = (
        P(("groups", "wide"), "narrow"),
        P(("groups", "wide"), "narrow"),
        P("narrow", "wide"),
        P("narrow", "wide"),
        P("narrow", "wide"),
        P("narrow", "wide"),
        P(("groups", "narrow")),
        P(("groups", "narrow")),
        P(),
    )
    return jax.shard_map(
        functools.partial(local, mesh.shape["wide"], mesh.shape["narrow"]),
        mesh=mesh,
        in_specs=placed,
        out_specs=(P(("groups", "narrow"), "wide"), P(("groups", "narrow"), "wide")),
        check_vma=False,
    )
```

profile of v0, /device:TPU:0, one launch (start us, length us, event | category | flops | bytes accessed | tf_op | source)
XLA Modules:
  0.0 47.8 jit_solution(9746649719019284732)
XLA Ops:
  0.6 45.4 %rescore.1 = (bf16[32,3584]{1,0:T(8,128)(2,1)}, bf16[32,3584]{1,0:T(8,128)(2,1)}) custom-call(s32[32]{0:T(128)} %ids_ref.1, s32[2]{0:T(128)} %len_ref.1, f32[128256]{0:T(1024)} %table_ref.1, bf16[32,2048]{1,0:T(8,128)(2,1)} %ts_ref.1, bf16[32,2048]{1,0:T(8,128)(2,1)} %ss_ref.1, bf16[2048,3584]{1,0:T(8,128)(2,1)} %tg_ref.1, bf16[2048,3584]{1,0:T(8,128)(2,1)} %tu_ref.1, ...), custom_call_target="tpu_custom_call" | custom-call | tf_op jit(solution)/shard_map/rescore/pallas_call | solution.py:287
  46.1 1.8 %hand_over.1 = (bf16[32,3584]{1,0:T(8,128)(2,1)}, bf16[32,3584]{1,0:T(8,128)(2,1)}) custom-call(bf16[32,3584]{1,0:T(8,128)(2,1)} %get-tuple-element.4.refs_0_, bf16[32,3584]{1,0:T(8,128)(2,1)} %get-tuple-element.5.refs_1_), custom_call_target="tpu_custom_call" | custom-call | tf_op jit(solution)/shard_map/hand_over/pallas_call | solution.py:319
where the time goes:
time: 48 us; the launch traced here: 47.8 us
  Pallas kernels  47.2 us (98%)
  between operations  0.64 us (1%)
    pallas_call x1, Pallas kernels, fused(): pl.pallas_call(functools.partial(kernel, wide, tn, slots), out_shape=(out...  45.4 us
    pallas_call x1, Pallas kernels, fused(): pl.pallas_call(hand_over, out_shape=(out, out), in_specs=[hbm, hbm], out_...  1.77 us

commit v1 on v0

v1 whole, which is shorter than its diff:
```python
import functools

import jax
import jax.numpy as jnp
from jax import lax
from jax.experimental import pallas as pl
from jax.experimental.pallas import tpu as pltpu
from jax.sharding import PartitionSpec as P

MESH = pl.DeviceIdType.MESH
VMEM_BYTES = 66_000_000
PIECES = (4, 2)
LAG = 2
AHEAD = (4, 3)
RELAYS = (
    (1, 2, 1, 0, 1), (3, 2, 1, 1, 1), (4, 2, 0, 0, 1), (6, 2, 0, 1, 1),
    (3, 1, 2, 0, -1), (4, 1, 2, 1, -1), (5, 1, 3, 0, -1), (6, 1, 3, 1, -1),
)


def matmul(left, right):
    return jnp.dot(left, right, preferred_element_type=jnp.float32)


def pair_project(w_gate, w_upper, piece):
    return jnp.concatenate([matmul(piece, w_gate), matmul(piece, w_upper)], axis=1)


def gated(summed, hidden_cols):
    return jax.nn.silu(summed[:, :hidden_cols]) * summed[:, hidden_cols:]


def kernel(
    tn, slots, ahead,
    ids_ref, len_ref, table_ref, ts_ref, ss_ref, tg_ref, tu_ref, sg_ref, su_ref,
    t_out, r_out,
    gath, wbuf, far_kept, near_kept, far_send, far_recv, near_send, near_recv, b_send, b_recv,
    kept, live_ref, weight_ref, table,
    table_sem, own_sem, g_send, g_recv, w_sem, fs_sem, fr_sem, ns_sem, nr_sem, bs_sem, br_sem,
):
    w = lax.axis_index("wide")
    n = lax.axis_index("narrow")
    x = n // 2
    c = n % 2
    mate = 2 * x + (1 - c)
    across = 2 * (1 - x) + c
    beside = 2 * (1 - x) + (1 - c)
    toward = 2 * x - 1
    v = x * w + (1 - x) * (3 - w)
    cols = tg_ref.shape[1]
    per = cols // tn
    units = 2 * per
    rows = gath.shape[2]
    depth = gath.shape[3]
    kept_slots = far_kept.shape[0]
    weights = ((tg_ref, tu_ref), (sg_ref, su_ref))

    def block(b):
        return x * b + (1 - x) * (3 - b)

    first = jnp.where(v == 0, block(0), block(1))
    second = jnp.where(v == 0, block(1), block(0))
    leads = across == first

    def weight_copies(u, model, j):
        span = pl.ds(pl.multiple_of(j * tn, tn), tn)
        return [
            pltpu.make_async_copy(weights[model][k].at[:, span], wbuf.at[u % slots, k], w_sem.at[u % slots, k])
            for k in range(2)
        ]

    def load(low, high):
        for u in range(low, high):
            for copy in weight_copies(u, u // per, u % per):
                copy.start()

    own = [
        pltpu.make_async_copy(ref, gath.at[m, w], own_sem.at[m])
        for m, ref in enumerate((ts_ref, ss_ref))
    ]
    for copy in own:
        copy.start()
    load(0, 2)

    barrier = pltpu.get_barrier_semaphore()

    def greet(axis, index):
        pl.semaphore_signal(barrier, inc=1, device_id={axis: index}, device_id_type=MESH)

    for gap in (-2, -1, 1, 2):
        @pl.when(jnp.logical_and(w + gap >= 0, w + gap <= 3))
        def _():
            greet("wide", w + gap)

    greet("narrow", mate)
    greet("narrow", across)
    inner = jnp.logical_and(w > 0, w < 3)
    pl.semaphore_wait(barrier, jnp.where(inner, 5, 4))

    def hop(m, b, p, step):
        size = depth // PIECES[m]
        part = gath.at[m, block(b), :, pl.ds(p * size, size)]
        way = {1: 0, -1: 1, 2: 2, -2: 2}[step]
        return pltpu.make_async_remote_copy(
            src_ref=part, dst_ref=part,
            send_sem=g_send.at[m, way, b, p], recv_sem=g_recv.at[m, b, p],
            device_id={"wide": w + toward * step}, device_id_type=MESH,
        )

    def send(m, b, *steps):
        for p in range(PIECES[m]):
            for step in steps:
                hop(m, b, p, step).start()

    def arrive(m, *blocks):
        for b in blocks:
            for p in range(PIECES[m]):
                hop(m, b, p, 1).wait_recv()

    def relay_piece(m, b, p, step):
        hop(m, b, p, 1).wait_recv()
        hop(m, b, p, step).start()

    def relay(m, b, step):
        for p in range(PIECES[m]):
            relay_piece(m, b, p, step)

    own[0].wait()

    @pl.when(v == 0)
    def _():
        send(0, 0, 1)
        send(0, 0, 2)

    @pl.when(v == 1)
    def _():
        send(0, 1, 1, -1)

    @pl.when(v == 2)
    def _():
        send(0, 2, -1, 1)

    @pl.when(v == 3)
    def _():
        send(0, 3, -1)
        send(0, 3, -2)

    own[1].wait()
    load(2, slots)
    fetch = pltpu.make_async_copy(table_ref, table, table_sem)
    fetch.start()

    @pl.when(v == 0)
    def _():
        send(1, 0, 2)
        send(1, 0, 1)

    @pl.when(v == 1)
    def _():
        relay(0, 2, -1)
        send(1, 1, 1)
        relay(0, 3, -1)
        send(1, 1, -1)

    @pl.when(v == 2)
    def _():
        relay(0, 1, 1)
        send(1, 2, -1)
        relay(0, 0, 1)

    @pl.when(v == 3)
    def _():
        send(1, 3, -2)
        send(1, 3, -1)
        arrive(0, 1)

    def relays(step):
        for at, where, b, p, way in RELAYS:
            @pl.when(jnp.logical_and(step == at, v == where))
            def _():
                relay_piece(1, b, p, way)

        @pl.when(jnp.logical_and(step == max(RELAYS)[0], v == 2))
        def _():
            send(1, 2, 1)

    def far_copy(u):
        return pltpu.make_async_remote_copy(
            src_ref=far_send.at[u], dst_ref=far_recv.at[u],
            send_sem=fs_sem.at[u], recv_sem=fr_sem.at[u],
            device_id={"narrow": mate}, device_id_type=MESH,
        )

    def near_copy(u):
        return pltpu.make_async_remote_copy(
            src_ref=near_send.at[u], dst_ref=near_recv.at[u],
            send_sem=ns_sem.at[u], recv_sem=nr_sem.at[u],
            device_id={"narrow": mate}, device_id_type=MESH,
        )

    def b_copy(u):
        return pltpu.make_async_remote_copy(
            src_ref=b_send.at[u], dst_ref=b_recv.at[u],
            send_sem=bs_sem.at[u], recv_sem=br_sem.at[u],
            device_id={"narrow": across}, device_id_type=MESH,
        )

    def cross(u):
        far_copy(u).wait_recv()
        for k in range(2):
            total = far_kept[u % kept_slots, k] + far_recv[u, k].astype(jnp.float32)
            b_send[u, k] = total.astype(jnp.bfloat16)
        b_copy(u).start()

    def tokens(model, *blocks):
        return jnp.concatenate([gath[model, i] for i in blocks], axis=0)

    def await_weights(u, model, j):
        for copy in weight_copies(u, model, j):
            copy.wait()

    def keep_far(u, k, out):
        far_kept[u % kept_slots, k] = out

    def give_far(u, k, out):
        far_send[u, k] = out.astype(jnp.bfloat16)

    def share_near(u, k, out):
        near_kept[u, k] = out[:rows]
        near_send[u, k] = out[rows:].astype(jnp.bfloat16)

    def refill(u):
        @pl.when(u + slots < units)
        def _():
            for copy in weight_copies(u + slots, 1, u + slots - per):
                copy.start()

    def phase(low, high, step0, body):
        def run(j, carry):
            relays(step0 + j - low)
            body(j)
            return carry
        lax.fori_loop(low, high, run, 0)
        return step0 + high - low

    def one_block(u, k, out, mine):
        @pl.when(mine)
        def _():
            keep_far(u, k, out)

        @pl.when(jnp.logical_not(mine))
        def _():
            give_far(u, k, out)

    def pass_on(u, mine):
        @pl.when(jnp.logical_not(mine))
        def _():
            far_copy(u).start()

        @pl.when(jnp.logical_and(mine, u >= LAG))
        def _():
            cross(u - LAG)

    def early(u):
        await_weights(u, 0, u)
        left = gath[0, first]
        for k in range(2):
            one_block(u, k, matmul(left, wbuf[u % slots, k]), leads)
        pass_on(u, leads)

    def rest(u):
        left = tokens(0, second, n, mate)
        for k in range(2):
            out = matmul(left, wbuf[u % slots, k])
            one_block(u, k, out[:rows], jnp.logical_not(leads))
            share_near(u, k, out[rows:])
        near_copy(u).start()
        pass_on(u, jnp.logical_not(leads))

        @pl.when(jnp.logical_and(leads, u < LAG))
        def _():
            cross(ahead[0] - LAG + u)

        refill(u)

    def whole(u, model):
        await_weights(u, model, u - model * per)
        left = tokens(model, across, beside, n, mate)
        for k in range(2):
            out = matmul(left, wbuf[u % slots, k])
            keep_far(u, k, out[:rows])
            give_far(u, k, out[rows:2 * rows])
            share_near(u, k, out[2 * rows:])
        far_copy(u).start()
        near_copy(u).start()

    def target(u):
        whole(u, 0)
        refill(u)

        @pl.when(jnp.logical_or(u >= ahead[0] + LAG, jnp.logical_not(leads)))
        def _():
            cross(u - LAG)

    def summed(u, k):
        near = near_kept[u, k] + near_recv[u, k].astype(jnp.float32)
        return near + b_recv[u, k].astype(jnp.float32)

    def activation(u):
        near_copy(u).wait_recv()
        b_copy(u).wait_recv()
        gate = summed(u, 0)
        return gate / (1.0 + jnp.exp(-gate)) * summed(u, 1)

    def finish_target(j):
        act = activation(j)
        kept[j] = act
        t_out[:, pl.ds(pl.multiple_of(j * tn, tn), tn)] = (live_ref[...] * act).astype(t_out.dtype)

    def finish_ratio(j, carry):
        act = activation(per + j)
        ratio = live_ref[...] * (kept[j] - weight_ref[...] * act)
        r_out[:, pl.ds(pl.multiple_of(j * tn, tn), tn)] = ratio.astype(r_out.dtype)
        return carry

    def source_far(j):
        u = per + j
        await_weights(u, 1, j)
        left = tokens(1, across, beside)
        for k in range(2):
            out = matmul(left, wbuf[u % slots, k])
            keep_far(u, k, out[:rows])
            give_far(u, k, out[rows:])
        far_copy(u).start()
        cross(u - LAG)

    def source_all(j):
        whole(per + j, 1)
        cross(per + j - LAG)
        finish_target(j - ahead[1])

    def source_near(j):
        u = per + j
        left = tokens(1, n, mate)
        for k in range(2):
            share_near(u, k, matmul(left, wbuf[u % slots, k]))
        near_copy(u).start()

        @pl.when(j < LAG)
        def _():
            cross(units - LAG + j)

        finish_target(per - ahead[1] + j)

    row = lax.broadcasted_iota(jnp.int32, (rows, 1), 0)
    hlen = rows // len_ref.shape[0]
    lived = jnp.zeros((rows, 1), jnp.float32)
    for h in range(len_ref.shape[0]):
        inside = jnp.logical_and(row >= h * hlen, row < h * hlen + len_ref[h])
        lived = jnp.where(inside, 1.0, lived)
    live_ref[...] = lived

    step = phase(0, ahead[0], 0, early)

    @pl.when(v == 0)
    def _():
        arrive(0, 1, 2, 3)

    @pl.when(v == 1)
    def _():
        arrive(0, 0)

    @pl.when(v == 2)
    def _():
        arrive(0, 3)

    @pl.when(v == 3)
    def _():
        arrive(0, 2, 0)

    step = phase(0, ahead[0], step, rest)
    step = phase(ahead[0], per, step, target)

    @pl.when(v == 0)
    def _():
        arrive(1, 1)

    @pl.when(v == 1)
    def _():
        arrive(1, 0)

    @pl.when(v == 3)
    def _():
        arrive(1, 1, 0)

    step = phase(0, ahead[1], step, source_far)

    @pl.when(v == 0)
    def _():
        arrive(1, 2, 3)

    @pl.when(v == 2)
    def _():
        arrive(1, 3)

    @pl.when(v == 3)
    def _():
        arrive(1, 2)

    step = phase(ahead[1], per, step, source_all)
    step = phase(0, ahead[1], step, source_near)

    fetch.wait()
    picked = jnp.zeros((rows, 1), jnp.float32)
    for i in range(rows):
        picked = jnp.where(row == i, table[ids_ref[i]], picked)
    weight_ref[...] = picked
    lax.fori_loop(0, per, finish_ratio, 0)

    def drain(u, carry):
        far_copy(u).wait_send()
        near_copy(u).wait_send()
        b_copy(u).wait_send()
        return carry

    lax.fori_loop(0, units, drain, 0)
    for m in range(2):
        for where, b, way in ((0, 0, 1), (0, 0, 2), (1, 1, 1), (1, 1, -1), (1, 2, -1), (1, 3, -1),
                              (2, 2, -1), (2, 2, 1), (2, 1, 1), (2, 0, 1), (3, 3, -1), (3, 3, -2)):
            @pl.when(v == where)
            def _():
                for p in range(PIECES[m]):
                    hop(m, b, p, way).wait_send()


def plan(states, weights, wide, narrow):
    depth, cols = weights.shape
    rows = states.shape[0]
    if narrow != 4 or wide != 4 or rows % 16 or depth % (128 * max(PIECES)):
        return None
    for tn in (512, 256):
        if cols % tn or cols // tn < 3:
            continue
        per = cols // tn
        ahead = [max(LAG, units * per // 7) for units in AHEAD]
        tile = rows * tn * 4
        fixed = 2 * wide * rows * depth * 2 + tile * (2 * per * (2 * 3 + 2) + 2 * (ahead[0] + LAG) + per)
        slots = (VMEM_BYTES - 1_500_000 - fixed) // (4 * tn * depth)
        slots = min(slots, 2 * per)
        if per - max(ahead) >= LAG and slots >= per + 2 and sum(ahead) + per > max(RELAYS)[0]:
            return tn, slots, ahead
    return None


def fused(states, weights, token_ids, lengths, ratio_weight, wide, tn, slots, ahead):
    rows, depth = states[0].shape
    cols = weights[0].shape[1]
    per = cols // tn
    units = 2 * per
    smem = pl.BlockSpec(memory_space=pltpu.SMEM)
    hbm = pl.BlockSpec(memory_space=pl.ANY)
    dma = pltpu.SemaphoreType.DMA
    wire = pltpu.VMEM((units, 2, rows, tn), jnp.bfloat16)
    held = pltpu.VMEM((rows, cols), jnp.bfloat16)
    vmem = pl.BlockSpec(memory_space=pltpu.VMEM)
    return pl.pallas_call(
        functools.partial(kernel, tn, slots, ahead),
        out_shape=(held, held),
        in_specs=[smem, smem] + [hbm] * 7,
        out_specs=(vmem, vmem),
        scratch_shapes=[
            pltpu.VMEM((2, wide, rows, depth), jnp.bfloat16),
            pltpu.VMEM((slots, 2, depth, tn), jnp.bfloat16),
            pltpu.VMEM((ahead[0] + LAG, 2, rows, tn), jnp.float32),
            pltpu.VMEM((units, 2, rows, tn), jnp.float32),
            wire, wire, wire, wire, wire, wire,
            pltpu.VMEM((per, rows, tn), jnp.float32),
            pltpu.VMEM((rows, 1), jnp.float32),
            pltpu.VMEM((rows, 1), jnp.float32),
            pltpu.SMEM(ratio_weight.shape, jnp.float32),
            dma,
            dma((2,)),
            dma((2, 3, wide, max(PIECES))),
            dma((2, wide, max(PIECES))),
            dma((slots, 2)),
            dma((units,)),
            dma((units,)),
            dma((units,)),
            dma((units,)),
            dma((units,)),
            dma((units,)),
        ],
        compiler_params=pltpu.CompilerParams(
            collective_id=0, has_side_effects=True, vmem_limit_bytes=VMEM_BYTES
        ),
        name="rescore",
    )(token_ids, lengths, ratio_weight, *states, *weights)


def local(
    wide,
    narrow,
    target_states,
    source_states,
    target_gate,
    target_up,
    source_gate,
    source_up,
    token_ids,
    lengths,
    ratio_weight,
):
    hidden_cols = target_gate.shape[1]
    own_rows = token_ids.shape[0]
    chosen = plan(target_states, target_gate, wide, narrow)
    if chosen is not None:
        return fused(
            (target_states, source_states),
            (target_gate, target_up, source_gate, source_up),
            token_ids,
            lengths,
            ratio_weight,
            wide,
            *chosen,
        )
    slot_count = own_rows // lengths.shape[0]
    slots = jnp.arange(slot_count, dtype=jnp.int32)
    live = (slots[None, :] < lengths[:, None]).reshape(-1).astype(jnp.float32)
    weight = ratio_weight[token_ids]
    target_terms = pair_project(
        target_gate, target_up, lax.all_gather(target_states, "wide", axis=0, tiled=True)
    )
    source_terms = pair_project(
        source_gate, source_up, lax.all_gather(source_states, "wide", axis=0, tiled=True)
    )
    target_sum, source_sum = (
        lax.psum_scatter(
            target_terms.astype(jnp.bfloat16), "narrow", scatter_dimension=0, tiled=True
        ).astype(jnp.float32),
        lax.psum_scatter(
            source_terms.astype(jnp.bfloat16), "narrow", scatter_dimension=0, tiled=True
        ).astype(jnp.float32),
    )
    target_act = gated(target_sum, hidden_cols)
    source_act = gated(source_sum, hidden_cols)
    target_out = (live[:, None] * target_act).astype(jnp.bfloat16)
    ratio_out = (live[:, None] * (target_act - weight[:, None] * source_act)).astype(jnp.bfloat16)
    return (target_out, ratio_out)


def solution(mesh):
    placed = (
        P(("groups", "wide"), "narrow"),
        P(("groups", "wide"), "narrow"),
        P("narrow", "wide"),
        P("narrow", "wide"),
        P("narrow", "wide"),
        P("narrow", "wide"),
        P(("groups", "narrow")),
        P(("groups", "narrow")),
        P(),
    )
    return jax.shard_map(
        functools.partial(local, mesh.shape["wide"], mesh.shape["narrow"]),
        mesh=mesh,
        in_specs=placed,
        out_specs=(P(("groups", "narrow"), "wide"), P(("groups", "narrow"), "wide")),
        check_vma=False,
    )
```

time: 48 us -> 45.9 us (0.956)
  Pallas kernels: 47.2 us -> 43.6 us
  local copies, waits for them, and re-layouts: 0 us -> 1.38 us
    pallas_call x2 -> x1, Pallas kernels: 47.2 us -> 43.6 us  [fused(): pl.pallas_call(functools.partial(kernel, tn, slots, ahead), out_shape=(he...]
    unnamed x0 -> x2, local copies, waits for them, and re-layouts: none -> 1.38 us
where the time goes in v1:
time: 45.9 us; the launch traced here: 45.6 us
  Pallas kernels  43.6 us (95%)
  local copies, waits for them, and re-layouts  1.38 us (3%)
  between operations  0.64 us (1%)
    pallas_call x1, Pallas kernels, fused(): pl.pallas_call(functools.partial(kernel, tn, slots, ahead), out_shape=(he...  43.6 us
    unnamed x2, local copies, waits for them, and re-layouts  1.38 us

profile of v1, /device:TPU:0, one launch (start us, length us, event | category | flops | bytes accessed | tf_op | source)
XLA Modules:
  0.0 45.6 jit_solution(1952450685654743248)
XLA Ops:
  0.6 43.6 %rescore.1 = (bf16[32,3584]{1,0:T(8,128)(2,1)S(1)}, bf16[32,3584]{1,0:T(8,128)(2,1)S(1)}) custom-call(s32[32]{0:T(128)} %ids_ref.1, s32[2]{0:T(128)} %len_ref.1, f32[128256]{0:T(1024)} %table_ref.1, bf16[32,2048]{1,0:T(8,128)(2,1)} %ts_ref.1, bf16[32,2048]{1,0:T(8,128)(2,1)} %ss_ref.1, bf16[2048,3584]{1,0:T(8,128)(2,1)} %tg_ref.1, ...), custom_call_target="tpu_custom_call" | custom-call | tf_op jit(solution)/shard_map/rescore/pallas_call | solution.py:466
  44.3 0.7 %copy.13 = bf16[32,3584]{1,0:T(8,128)(2,1)} copy(bf16[32,3584]{1,0:T(8,128)(2,1)S(1)} %get-tuple-element.2) | data formatting | bytes 458752
  44.9 0.7 %copy.14 = bf16[32,3584]{1,0:T(8,128)(2,1)} copy(bf16[32,3584]{1,0:T(8,128)(2,1)S(1)} %get-tuple-element.3) | data formatting | bytes 458752

commit v2 on v1

--- a/solution.py
+++ b/solution.py
@@ -13,8 +13,8 @@
 LAG = 2
 AHEAD = (4, 3)
 RELAYS = (
-    (1, 2, 1, 0, 1), (3, 2, 1, 1, 1), (4, 2, 0, 0, 1), (6, 2, 0, 1, 1),
-    (3, 1, 2, 0, -1), (4, 1, 2, 1, -1), (5, 1, 3, 0, -1), (6, 1, 3, 1, -1),
+    (0, 2, 1, 0, 1), (1, 2, 1, 1, 1), (2, 2, 0, 0, 1), (3, 2, 0, 1, 1),
+    (1, 1, 2, 0, -1), (2, 1, 2, 1, -1), (3, 1, 3, 0, -1), (4, 1, 3, 1, -1),
 )
 
 

time: 45.9 us -> 47.2 us (1.028)
  the two profiles are of different devices: /device:TPU:0 before, /device:TPU:8 now
where the time goes in v2:
time: 47.2 us; the launch traced here: 47 us
  Pallas kernels  45 us (95%)
  local copies, waits for them, and re-layouts  1.38 us (3%)
  between operations  0.64 us (1%)
    pallas_call x1, Pallas kernels, fused(): pl.pallas_call(functools.partial(kernel, tn, slots, ahead), out_shape=(he...  45 us
    unnamed x2, local copies, waits for them, and re-layouts  1.38 us

profile of v2, /device:TPU:8, one launch (start us, length us, event | category | flops | bytes accessed | tf_op | source)
XLA Modules:
  0.0 47.0 jit_solution(2612593870942416014)
XLA Ops:
  0.6 45.0 %rescore.1 = (bf16[32,3584]{1,0:T(8,128)(2,1)S(1)}, bf16[32,3584]{1,0:T(8,128)(2,1)S(1)}) custom-call(s32[32]{0:T(128)} %ids_ref.1, s32[2]{0:T(128)} %len_ref.1, f32[128256]{0:T(1024)} %table_ref.1, bf16[32,2048]{1,0:T(8,128)(2,1)} %ts_ref.1, bf16[32,2048]{1,0:T(8,128)(2,1)} %ss_ref.1, bf16[2048,3584]{1,0:T(8,128)(2,1)} %tg_ref.1, ...), custom_call_target="tpu_custom_call" | custom-call | tf_op jit(solution)/shard_map/rescore/pallas_call | solution.py:466
  45.7 0.7 %copy.13 = bf16[32,3584]{1,0:T(8,128)(2,1)} copy(bf16[32,3584]{1,0:T(8,128)(2,1)S(1)} %get-tuple-element.2) | data formatting | bytes 458752
  46.4 0.7 %copy.14 = bf16[32,3584]{1,0:T(8,128)(2,1)} copy(bf16[32,3584]{1,0:T(8,128)(2,1)S(1)} %get-tuple-element.3) | data formatting | bytes 458752

commit v3 on v2

--- a/solution.py
+++ b/solution.py
@@ -13,8 +13,10 @@
 LAG = 2
 AHEAD = (4, 3)
 RELAYS = (
-    (0, 2, 1, 0, 1), (1, 2, 1, 1, 1), (2, 2, 0, 0, 1), (3, 2, 0, 1, 1),
-    (1, 1, 2, 0, -1), (2, 1, 2, 1, -1), (3, 1, 3, 0, -1), (4, 1, 3, 1, -1),
+    (0, 1, 0, 3, 0, -1), (1, 1, 0, 3, 1, -1), (2, 1, 0, 3, 2, -1), (3, 1, 0, 3, 3, -1),
+    (0, 2, 0, 0, 0, 1), (1, 2, 0, 0, 1, 1), (2, 2, 0, 0, 2, 1), (3, 2, 0, 0, 3, 1),
+    (5, 2, 1, 1, 0, 1), (6, 2, 1, 1, 1, 1), (7, 2, 1, 0, 0, 1), (8, 2, 1, 0, 1, 1),
+    (5, 1, 1, 2, 0, -1), (6, 1, 1, 2, 1, -1), (7, 1, 1, 3, 0, -1), (8, 1, 1, 3, 1, -1),
 )
 
 
@@ -159,14 +161,11 @@
     def _():
         relay(0, 2, -1)
         send(1, 1, 1)
-        relay(0, 3, -1)
-        send(1, 1, -1)
 
     @pl.when(v == 2)
     def _():
         relay(0, 1, 1)
         send(1, 2, -1)
-        relay(0, 0, 1)
 
     @pl.when(v == 3)
     def _():
@@ -175,12 +174,16 @@
         arrive(0, 1)
 
     def relays(step):
-        for at, where, b, p, way in RELAYS:
+        for at, where, m, b, p, way in RELAYS:
             @pl.when(jnp.logical_and(step == at, v == where))
             def _():
-                relay_piece(1, b, p, way)
-
-        @pl.when(jnp.logical_and(step == max(RELAYS)[0], v == 2))
+                relay_piece(m, b, p, way)
+
+        @pl.when(jnp.logical_and(step == PIECES[0], v == 1))
+        def _():
+            send(1, 1, -1)
+
+        @pl.when(jnp.logical_and(step == 8, v == 2))
         def _():
             send(1, 2, 1)
 
@@ -447,7 +450,7 @@
         fixed = 2 * wide * rows * depth * 2 + tile * (2 * per * (2 * 3 + 2) + 2 * (ahead[0] + LAG) + per)
         slots = (VMEM_BYTES - 1_500_000 - fixed) // (4 * tn * depth)
         slots = min(slots, 2 * per)
-        if per - max(ahead) >= LAG and slots >= per + 2 and sum(ahead) + per > max(RELAYS)[0]:
+        if per - max(ahead) >= LAG and slots >= per + 2 and ahead[0] >= PIECES[0] and ahead[0] + per > max(RELAYS)[0]:
             return tn, slots, ahead
     return None
 

time: 47.2 us -> 47.2 us (level)
  the two profiles are of different devices: /device:TPU:8 before, /device:TPU:0 now
where the time goes in v3:
time: 47.2 us; the launch traced here: 47 us
  Pallas kernels  45 us (95%)
  local copies, waits for them, and re-layouts  1.38 us (3%)
  between operations  0.64 us (1%)
    pallas_call x1, Pallas kernels, fused(): pl.pallas_call(functools.partial(kernel, tn, slots, ahead), out_shape=(he...  45 us
    unnamed x2, local copies, waits for them, and re-layouts  1.38 us

profile of v3, /device:TPU:0, one launch (start us, length us, event | category | flops | bytes accessed | tf_op | source)
XLA Modules:
  0.0 47.0 jit_solution(13544583406478613863)
XLA Ops:
  0.6 45.0 %rescore.1 = (bf16[32,3584]{1,0:T(8,128)(2,1)S(1)}, bf16[32,3584]{1,0:T(8,128)(2,1)S(1)}) custom-call(s32[32]{0:T(128)} %ids_ref.1, s32[2]{0:T(128)} %len_ref.1, f32[128256]{0:T(1024)} %table_ref.1, bf16[32,2048]{1,0:T(8,128)(2,1)} %ts_ref.1, bf16[32,2048]{1,0:T(8,128)(2,1)} %ss_ref.1, bf16[2048,3584]{1,0:T(8,128)(2,1)} %tg_ref.1, ...), custom_call_target="tpu_custom_call" | custom-call | tf_op jit(solution)/shard_map/rescore/pallas_call | solution.py:469
  45.6 0.7 %copy.13 = bf16[32,3584]{1,0:T(8,128)(2,1)} copy(bf16[32,3584]{1,0:T(8,128)(2,1)S(1)} %get-tuple-element.2) | data formatting | bytes 458752
  46.3 0.7 %copy.14 = bf16[32,3584]{1,0:T(8,128)(2,1)} copy(bf16[32,3584]{1,0:T(8,128)(2,1)S(1)} %get-tuple-element.3) | data formatting | bytes 458752

commit v4 on v2

--- a/solution.py
+++ b/solution.py
@@ -11,10 +11,10 @@
 VMEM_BYTES = 66_000_000
 PIECES = (4, 2)
 LAG = 2
-AHEAD = (4, 3)
+AHEAD = (4, 2)
 RELAYS = (
-    (0, 2, 1, 0, 1), (1, 2, 1, 1, 1), (2, 2, 0, 0, 1), (3, 2, 0, 1, 1),
-    (1, 1, 2, 0, -1), (2, 1, 2, 1, -1), (3, 1, 3, 0, -1), (4, 1, 3, 1, -1),
+    (2, 2, 1, 0, 1), (4, 2, 1, 1, 1), (5, 2, 0, 0, 1), (7, 2, 0, 1, 1),
+    (4, 1, 2, 0, -1), (5, 1, 2, 1, -1), (6, 1, 3, 0, -1), (7, 1, 3, 1, -1),
 )
 
 

time: 47.2 us -> 45.9 us (0.972)
  the two profiles are of different devices: /device:TPU:8 before, /device:TPU:0 now
where the time goes in v4:
time: 45.9 us; the launch traced here: 45.6 us
  Pallas kernels  43.6 us (95%)
  local copies, waits for them, and re-layouts  1.38 us (3%)
  between operations  0.64 us (1%)
    pallas_call x1, Pallas kernels, fused(): pl.pallas_call(functools.partial(kernel, tn, slots, ahead), out_shape=(he...  43.6 us
    unnamed x2, local copies, waits for them, and re-layouts  1.38 us

profile of v4, /device:TPU:0, one launch (start us, length us, event | category | flops | bytes accessed | tf_op | source)
XLA Modules:
  0.0 45.6 jit_solution(17891493609434158687)
XLA Ops:
  0.6 43.6 %rescore.1 = (bf16[32,3584]{1,0:T(8,128)(2,1)S(1)}, bf16[32,3584]{1,0:T(8,128)(2,1)S(1)}) custom-call(s32[32]{0:T(128)} %ids_ref.1, s32[2]{0:T(128)} %len_ref.1, f32[128256]{0:T(1024)} %table_ref.1, bf16[32,2048]{1,0:T(8,128)(2,1)} %ts_ref.1, bf16[32,2048]{1,0:T(8,128)(2,1)} %ss_ref.1, bf16[2048,3584]{1,0:T(8,128)(2,1)} %tg_ref.1, ...), custom_call_target="tpu_custom_call" | custom-call | tf_op jit(solution)/shard_map/rescore/pallas_call | solution.py:466
  44.3 0.7 %copy.13 = bf16[32,3584]{1,0:T(8,128)(2,1)} copy(bf16[32,3584]{1,0:T(8,128)(2,1)S(1)} %get-tuple-element.2) | data formatting | bytes 458752
  44.9 0.7 %copy.14 = bf16[32,3584]{1,0:T(8,128)(2,1)} copy(bf16[32,3584]{1,0:T(8,128)(2,1)S(1)} %get-tuple-element.3) | data formatting | bytes 458752
